TPU v7x, 32 devices: a whole 2x2x4 slice. The times are simulated.
32 devices in a mesh: groups: 2 (over y), row: 4 (over z), col: 4 (over x, core).
Axes of the slice: x: 2, y: 2, z: 4, core: 2. Of those that a mesh axis runs over, the one named last changes fastest.
Arguments:
- prev_solution: float32 [16384, 1024], P(None, ('groups', 'row', 'col')), parts along dimension 1, may hold values from -6 to 6
- factor_panel: float32 [1024, 16384], P(None, ('row', 'col')), may hold values from -0.0625 to 0.0625
- right_side: float32 [1024, 1024], P('row', ('groups', 'col')), parts along dimension 1, may hold values from -6 to 6
- window_factor: float32 [1024, 1024], P('row'), may hold values from -2 to 2, as said below
Outputs:
- window_solution: float32 [1024, 1024], P('row', ('groups', 'col')), parts along dimension 1
There are 2 independent parts, one for each index of `groups`. A program takes and returns all parts, laid end to end along the dimension named above; an argument that names none is the same for every part. Nothing has to cross between parts.
Inputs may be any that keep to these rules, and one draw needn't show every extreme that they name: `window_factor`: lower triangular, with diagonal entries between 1 and 2.
All inputs are finite; a program needn't handle non-finite values.
Results may differ from a plain program's by a relative error of at most 0.0003.
Values sent between devices are 32-bit elements; how exact they have to be, the bound alone decides.
No kernel may reach another device: no remote copies, remote signals or barrier semaphores. Data moves between devices by JAX's collectives and lax.ppermute only.
A program may use at most 64 MiB of HBM per device.

v0:
```python
import jax
import jax.numpy as jnp
from jax import lax
from jax.sharding import PartitionSpec as P


def broadcast(value, axis, root):
    mine = lax.axis_index(axis) == root
    return lax.psum(jnp.where(mine, value, jnp.zeros_like(value)), axis)


def shards(prev_solution, factor_panel, right_side, window_factor):
    highest = lax.Precision.HIGHEST
    row_count = lax.axis_size("row")
    row_index = lax.axis_index("row")
    strip_rows = right_side.shape[0]
    by_rows = lax.all_to_all(prev_solution, ("row", "col"), split_axis=0, concat_axis=1, tiled=True)
    row_summed = lax.psum_scatter(
        jnp.dot(factor_panel, by_rows, precision=highest, preferred_element_type=jnp.float32),
        "row",
        scatter_dimension=0,
        tiled=True,
    )
    coupling = lax.psum_scatter(row_summed, "col", scatter_dimension=1, tiled=True)
    residual = right_side - coupling
    own_block = lax.dynamic_slice_in_dim(window_factor, row_index * strip_rows, strip_rows, 1)

    def sweep_step(strip_index, state_pair):
        pending, solved = state_pair
        candidate = jax.scipy.linalg.solve_triangular(own_block, pending, lower=True)
        arrived = broadcast(candidate, "row", strip_index)
        column_block = lax.dynamic_slice_in_dim(
            window_factor, strip_index * strip_rows, strip_rows, 1
        )
        update = jnp.dot(
            column_block, arrived, precision=highest, preferred_element_type=jnp.float32
        )
        pending = jnp.where(row_index > strip_index, pending - update, pending)
        solved = jnp.where(row_index == strip_index, arrived, solved)
        return (pending, solved)

    pending, solved = lax.fori_loop(0, row_count, sweep_step, (residual, jnp.zeros_like(residual)))
    return solved


def solution(mesh):
    in_specs = (
        P(None, ("groups", "row", "col")),
        P(None, ("row", "col")),
        P("row", ("groups", "col")),
        P("row", None),
    )
    out_specs = P("row", ("groups", "col"))
    return jax.shard_map(shards, mesh=mesh, in_specs=in_specs, out_specs=out_specs, check_vma=False)
```

profile of v0, /device:TPU:0, one launch (start us, length us, event | category | flops | bytes accessed | tf_op | source)
XLA Modules:
  0.0 303.0 jit_solution(4795972882912780716)
XLA Ops:
  6.5 1.7 copy.13
  8.3 54.7 %all_to_all.19 = f32[16,1024,32]{1,2,0:T(8,128)S(1)} all-to-all(f32[16,1024,32]{1,2,0:T(8,128)S(1)} %bitcast.42), channel_id=1, replica_groups=mesh['groups'=2,'row'=4,'col'=4] {'row','col'}, dimensions={0} | all-to-all | bytes 4194304 | tf_op jit(solution)/shard_map/all_to_all | solution.py:17
  63.0 8.1 %fusion.17 = f32[1024,512]{1,0:T(8,128)} fusion(f32[1024,1024]{1,0:T(8,128)S(1)} %copy-done, f32[1024,512]{0,1:T(8,128)S(1)} %bitcast.43), kind=kOutput, calls=%fused_computation.30 | convolution fusion | flops 6442450944 | bytes 8388608 | tf_op jit(solution)/shard_map/dot_general | solution.py:19
  71.2 44.4 %reduce-scatter.3.cloned.1.call-done = f32[256,512]{1,0:T(8,128)} async-done(((f32[1024,512]{1,0:T(8,128)}), f32[256,512]{1,0:T(8,128)}) %reduce-scatter.3.cloned.1.call-update) | async-done | bytes 524304 | tf_op jit(solution)/shard_map/reduce_scatter | solution.py:18
  115.8 4.3 %while.20 = (s32[]{:T(128)}, f32[256,256]{1,0:T(8,128)S(1)}, s32[2,2]{1,0:T(2,128)S(1)}, f32[2,128,128]{2,1,0:T(8,128)S(1)}, s32[]{:T(128)}) while((s32[]{:T(128)}, f32[256,256]{1,0:T(8,128)S(1)}, s32[2,2]{1,0:T(2,128)S(1)}, f32[2,128,128]{2,1,0:T(8,128)S(1)}, s32[]{:T(128)}) %tuple.62), condition=%wide.while_cond, body=%wide.while_body.sunk | while | flops 2 | bytes 131189 | solution.py:30
  115.8 0.7 fusion.33
  116.5 1.5 bitcast_dynamic-update-slice_fusion.2
  118.0 0.7 fusion.33
  118.6 1.5 bitcast_dynamic-update-slice_fusion.2
  120.1 19.7 %custom-call.11 = f32[2,128,128]{1,2,0:T(8,128)S(1)} custom-call(f32[2,128,128]{2,1,0:T(8,128)S(1)} %get-tuple-element.195), custom_call_target="InvertDiagBlocksLowerTriangular" | custom-call | tf_op jit(solution)/shard_map/while/body/eval_jaxpr/jit(_solve_triangular)/triangular_solve | solution.py:30
  139.9 0.9 sub.13
  140.8 154.7 %while.21 = (s32[]{:T(128)}, f32[256,128]{1,0:T(8,128)S(1)}, f32[256,128]{1,0:T(8,128)S(1)}, s32[]{:T(128)}, f32[256,1024]{1,0:T(8,128)S(1)}, /*index=5*/f32[2,1...) while((s32[]{:T(128)}, f32[256,128]{1,0:T(8,128)S(1)}, ...), condition=%wide.region_4.5_spmd.clone, body=%wide.region_2.4_spmd.clone.sunk | while | flops 176472064 | bytes 2752807 | solution.py:42
  140.9 0.2 fusion.41
  141.1 0.2 convolution_subtract_fusion.3
  141.3 0.2 convolution_bitcast_fusion.2
  141.6 0.7 maximum_select_fusion.2
  142.3 35.6 %all-reduce.2.cloned.1.call-done = f32[256,128]{1,0:T(8,128)} async-done(((f32[256,128]{1,0:T(8,128)}), f32[256,128]{1,0:T(8,128)}) %all-reduce.2.cloned.1.call-update) | async-done | bytes 131088 | tf_op jit(solution)/shard_map/while/body/eval_jaxpr/psum | solution.py:9
  177.9 1.3 fusion.42
  179.2 0.9 select_select_fusion.2
  180.5 0.2 convolution_subtract_fusion.3
  180.9 0.7 maximum_select_fusion.2
  181.6 34.7 %all-reduce.2.cloned.1.call-done = f32[256,128]{1,0:T(8,128)} async-done(((f32[256,128]{1,0:T(8,128)}), f32[256,128]{1,0:T(8,128)}) %all-reduce.2.cloned.1.call-update) | async-done | bytes 131088 | tf_op jit(solution)/shard_map/while/body/eval_jaxpr/psum | solution.py:9
  216.3 1.3 fusion.42
  218.1 0.2 convolution_bitcast_fusion.2
  218.4 0.7 maximum_select_fusion.2
  219.1 35.8 %all-reduce.2.cloned.1.call-done = f32[256,128]{1,0:T(8,128)} async-done(((f32[256,128]{1,0:T(8,128)}), f32[256,128]{1,0:T(8,128)}) %all-reduce.2.cloned.1.call-update) | async-done | bytes 131088 | tf_op jit(solution)/shard_map/while/body/eval_jaxpr/psum | solution.py:9
  254.9 1.3 fusion.42
  256.7 0.2 convolution_bitcast_fusion.2
  257.0 0.7 maximum_select_fusion.2
  257.7 36.4 %all-reduce.2.cloned.1.call-done = f32[256,128]{1,0:T(8,128)} async-done(((f32[256,128]{1,0:T(8,128)}), f32[256,128]{1,0:T(8,128)}) %all-reduce.2.cloned.1.call-update) | async-done | bytes 131088 | tf_op jit(solution)/shard_map/while/body/eval_jaxpr/psum | solution.py:9
  294.1 1.3 fusion.42
  295.5 0.6 copy-done.1
  (37 shorter events, 1.9 us)
Async XLA Ops:
  6.5 109.1 %reduce-scatter.3.cloned.1.call-start = ((), (), s32[]{:S(2)}) async-start(), calls=%async_computation.3 | async-start | bytes 2621440 | tf_op jit(solution)/shard_map/reduce_scatter | solution.py:18
  8.3 54.8 %copy-start = (f32[1024,1024]{1,0:T(8,128)S(1)}, f32[1024,1024]{1,0:T(8,128)}, u32[]{:S(2)}) copy-start(f32[1024,1024]{1,0:T(8,128)} %param.7) | copy-start | bytes 12582916
  71.1 44.6 %copy-start.2 = (f32[256,1024]{1,0:T(8,128)S(1)}, f32[256,1024]{1,0:T(8,128)}, u32[]{:S(2)}) copy-start(f32[256,1024]{1,0:T(8,128)} %param.9) | copy-start | bytes 3145732
  71.1 68.8 %copy-start.3 = (f32[256,128]{1,0:T(8,128)S(1)}, f32[256,128]{1,0:T(8,128)}, u32[]{:S(2)}) copy-start(f32[256,128]{1,0:T(8,128)} %param.8) | copy-start | bytes 393220
  71.1 68.8 %reduce-scatter.5.cloned.1.call-start = ((), (), s32[]{:S(2)}) async-start(), calls=%async_computation.4 | async-start | bytes 655360 | tf_op jit(solution)/shard_map/reduce_scatter | solution.py:24
  140.9 37.0 %all-reduce.2.cloned.1.call-start = ((), (), s32[]{:S(2)}) async-start(), calls=%async_computation.5 | async-start | bytes 262144 | tf_op jit(solution)/shard_map/while/body/eval_jaxpr/psum | solution.py:9
  180.2 36.1 %all-reduce.2.cloned.1.call-start = ((), (), s32[]{:S(2)}) async-start(), calls=%async_computation.5 | async-start | bytes 262144 | tf_op jit(solution)/shard_map/while/body/eval_jaxpr/psum | solution.py:9
  217.7 37.2 %all-reduce.2.cloned.1.call-start = ((), (), s32[]{:S(2)}) async-start(), calls=%async_computation.5 | async-start | bytes 262144 | tf_op jit(solution)/shard_map/while/body/eval_jaxpr/psum | solution.py:9
  256.3 37.9 %all-reduce.2.cloned.1.call-start = ((), (), s32[]{:S(2)}) async-start(), calls=%async_computation.5 | async-start | bytes 262144 | tf_op jit(solution)/shard_map/while/body/eval_jaxpr/psum | solution.py:9
  295.5 0.7 copy-start.1
Sparse Core Ops, SparseCore 0:
  71.2 44.3 reduce-scatter.2
  118.2 21.0 reduce-scatter.4
  144.0 33.8 all-reduce.1
  183.0 33.1 all-reduce.1
  220.5 34.3 all-reduce.1
  259.1 34.9 all-reduce.1
where the time goes:
time: 303 us
  waiting for transfers between devices  187 us (62%)
  blocking collectives  54.7 us (18%)
  other arithmetic  24.4 us (8%)
  matrix products  15.8 us (5%)
  between operations  13.5 us (4%)
  local copies, waits for them, and re-layouts  6.83 us (2%)
    psum x4, waiting for transfers between devices, broadcast(): return lax.psum(jnp.where(mine, value, jnp.zeros_like(value)), axis)  143 us
    all_to_all x1, blocking collectives, shards(): lax.all_to_all(prev_solution, ('row', 'col'), split_axis=0, concat_axis=1...  54.7 us
    reduce_scatter x1, waiting for transfers between devices, shards(): lax.psum_scatter(jnp.dot(factor_panel, by_rows, precision=highest, prefer...  44.4 us
    another operation x3, other arithmetic, sweep_step(): jax.scipy.linalg.solve_triangular(own_block, pending, lower=True)  19.7 us
    dot_general x1, matrix products, shards(): jnp.dot(factor_panel, by_rows, precision=highest, preferred_element_type=...  8.05 us
  transfers between devices with their start and end apart: 6, of which 5 were waited for; matrix products, arithmetic and copies ran while one was open for 8% of the time, Pallas kernels for 0%

commit v1 on v0

--- a/solution.py
+++ b/solution.py
@@ -6,7 +6,7 @@
 
 def broadcast(value, axis, root):
     mine = lax.axis_index(axis) == root
-    return lax.psum(jnp.where(mine, value, jnp.zeros_like(value)), axis)
+    return jnp.sum(lax.all_gather(jnp.where(mine, value, jnp.zeros_like(value)), axis), axis=0)
 
 
 def shards(prev_solution, factor_panel, right_side, window_factor):

time: 303 us -> 216 us (0.71)
  waiting for transfers between devices: 187 us -> 44.5 us
  blocking collectives: 54.7 us -> 117 us
  matrix products: 15.8 us -> 12.2 us
  other arithmetic: 24.4 us -> 20.9 us
    psum x4 -> x0, waiting for transfers between devices: 143 us -> none  [broadcast(): return lax.psum(jnp.where(mine, value, jnp.zeros_like(value)), axis)]
    all_gather x0 -> x4, blocking collectives: none -> 62.5 us  [broadcast(): lax.all_gather(jnp.where(mine, value, jnp.zeros_like(value)), axis)]
    dot_general x4, matrix products: 5.28 us -> 1.68 us  [sweep_step(): jnp.dot(column_block, arrived, precision=highest, preferred_element_type=...]
  transfers between devices with their start and end apart: 6 -> 2, of which waited for: 5 -> 1; matrix products, arithmetic and copies ran while one was open for 8% -> 11% of each run, Pallas kernels for 0% -> 0%
where the time goes in v1:
time: 216 us; the launch traced here: 215 us
  blocking collectives  117 us (54%)
  waiting for transfers between devices  44.5 us (21%)
  other arithmetic  20.9 us (10%)
  between operations  13.5 us (6%)
  matrix products  12.2 us (6%)
  local copies, waits for them, and re-layouts  6.52 us (3%)
    all_gather x4, blocking collectives, broadcast(): lax.all_gather(jnp.where(mine, value, jnp.zeros_like(value)), axis)  62.5 us
    all_to_all x1, blocking collectives, shards(): lax.all_to_all(prev_solution, ('row', 'col'), split_axis=0, concat_axis=1...  54.7 us
    reduce_scatter x1, waiting for transfers between devices, shards(): lax.psum_scatter(jnp.dot(factor_panel, by_rows, precision=highest, prefer...  44.4 us
    another operation x3, other arithmetic, sweep_step(): jax.scipy.linalg.solve_triangular(own_block, pending, lower=True)  19.7 us
    dot_general x1, matrix products, shards(): jnp.dot(factor_panel, by_rows, precision=highest, preferred_element_type=...  8.05 us
  transfers between devices with their start and end apart: 2, of which 1 were waited for; matrix products, arithmetic and copies ran while one was open for 11% of the time, Pallas kernels for 0%

profile of v1, /device:TPU:0, one launch (start us, length us, event | category | flops | bytes accessed | tf_op | source)
XLA Modules:
  0.0 215.4 jit_solution(9563377245543030978)
XLA Ops:
  6.5 1.7 copy.13
  8.3 54.7 %all_to_all.19 = f32[16,1024,32]{1,2,0:T(8,128)S(1)} all-to-all(f32[16,1024,32]{1,2,0:T(8,128)S(1)} %bitcast.48), channel_id=1, replica_groups=mesh['groups'=2,'row'=4,'col'=4] {'row','col'}, dimensions={0} | all-to-all | bytes 4194304 | tf_op jit(solution)/shard_map/all_to_all | solution.py:17
  63.0 8.1 %fusion.17 = f32[1024,512]{1,0:T(8,128)} fusion(f32[1024,1024]{1,0:T(8,128)S(1)} %copy-done, f32[1024,512]{0,1:T(8,128)S(1)} %bitcast.49), kind=kOutput, calls=%fused_computation.30 | convolution fusion | flops 6442450944 | bytes 8388608 | tf_op jit(solution)/shard_map/dot_general | solution.py:19
  71.1 44.4 %reduce-scatter.3.cloned.1.call-done = f32[256,512]{1,0:T(8,128)} async-done(((f32[1024,512]{1,0:T(8,128)}), f32[256,512]{1,0:T(8,128)}) %reduce-scatter.3.cloned.1.call-update) | async-done | bytes 524304 | tf_op jit(solution)/shard_map/reduce_scatter | solution.py:18
  115.8 4.0 %while.20 = (s32[]{:T(128)}, f32[256,256]{1,0:T(8,128)S(1)}, s32[2,2]{1,0:T(2,128)S(1)}, f32[2,128,128]{2,1,0:T(8,128)S(1)}, s32[]{:T(128)}) while((s32[]{:T(128)}, f32[256,256]{1,0:T(8,128)S(1)}, s32[2,2]{1,0:T(2,128)S(1)}, f32[2,128,128]{2,1,0:T(8,128)S(1)}, s32[]{:T(128)}) %tuple.62), condition=%wide.while_cond, body=%wide.while_body.sunk | while | flops 2 | bytes 131189 | solution.py:30
  115.8 0.6 fusion.33
  116.4 1.4 bitcast_dynamic-update-slice_fusion.2
  117.8 0.6 fusion.33
  118.4 1.4 bitcast_dynamic-update-slice_fusion.2
  119.8 19.7 %custom-call.11 = f32[2,128,128]{1,2,0:T(8,128)S(1)} custom-call(f32[2,128,128]{2,1,0:T(8,128)S(1)} %get-tuple-element.195), custom_call_target="InvertDiagBlocksLowerTriangular" | custom-call | tf_op jit(solution)/shard_map/while/body/eval_jaxpr/jit(_solve_triangular)/triangular_solve | solution.py:30
  139.6 0.9 sub.13
  140.5 67.3 %while.21 = (s32[]{:T(128)}, f32[256,128]{1,0:T(8,128)S(1)}, f32[256,128]{1,0:T(8,128)S(1)}, s32[]{:T(128)}, f32[256,1024]{1,0:T(8,128)S(1)}, /*index=5*/f32[2,1...) while((s32[]{:T(128)}, f32[256,128]{1,0:T(8,128)S(1)}, ...), condition=%wide.region_4.5_spmd.clone, body=%wide.region_2.4_spmd.clone.sunk | while | flops 176537600 | bytes 3277067 | solution.py:42
  140.5 0.2 fusion.41
  140.8 0.2 convolution_subtract_fusion.3
  141.0 0.2 convolution_bitcast_fusion.2
  141.2 15.4 %all_gather.15 = f32[4,256,128]{2,1,0:T(8,128)S(1)} all-gather(f32[1,256,128]{2,1,0:T(8,128)S(1)} %maximum_select_fusion.2), channel_id=1, replica_groups=mesh['groups'=2,'row'=4,'col'=4] {'row'}, dimensions={0}, use_global_device_ids=true | all-gather | bytes 655360 | tf_op jit(solution)/shard_map/while/body/eval_jaxpr/all_gather | solution.py:9
  156.7 0.4 fusion.42
  157.2 0.2 fusion.41
  157.4 0.2 convolution_subtract_fusion.3
  157.6 0.2 convolution_bitcast_fusion.2
  157.8 16.2 %all_gather.15 = f32[4,256,128]{2,1,0:T(8,128)S(1)} all-gather(f32[1,256,128]{2,1,0:T(8,128)S(1)} %maximum_select_fusion.2), channel_id=1, replica_groups=mesh['groups'=2,'row'=4,'col'=4] {'row'}, dimensions={0}, use_global_device_ids=true | all-gather | bytes 655360 | tf_op jit(solution)/shard_map/while/body/eval_jaxpr/all_gather | solution.py:9
  174.1 0.4 fusion.42
  174.6 0.2 fusion.41
  174.8 0.2 convolution_subtract_fusion.3
  175.3 16.2 %all_gather.15 = f32[4,256,128]{2,1,0:T(8,128)S(1)} all-gather(f32[1,256,128]{2,1,0:T(8,128)S(1)} %maximum_select_fusion.2), channel_id=1, replica_groups=mesh['groups'=2,'row'=4,'col'=4] {'row'}, dimensions={0}, use_global_device_ids=true | all-gather | bytes 655360 | tf_op jit(solution)/shard_map/while/body/eval_jaxpr/all_gather | solution.py:9
  191.5 0.4 fusion.42
  192.0 0.2 fusion.41
  192.2 0.2 convolution_subtract_fusion.3
  192.4 0.2 convolution_bitcast_fusion.2
  192.6 14.7 %all_gather.15 = f32[4,256,128]{2,1,0:T(8,128)S(1)} all-gather(f32[1,256,128]{2,1,0:T(8,128)S(1)} %maximum_select_fusion.2), channel_id=1, replica_groups=mesh['groups'=2,'row'=4,'col'=4] {'row'}, dimensions={0}, use_global_device_ids=true | all-gather | bytes 655360 | tf_op jit(solution)/shard_map/while/body/eval_jaxpr/all_gather | solution.py:9
  207.4 0.4 fusion.42
  207.9 0.6 copy-done.1
  (33 shorter events, 0.8 us)
Async XLA Ops:
  6.5 109.0 %reduce-scatter.3.cloned.1.call-start = ((), (), s32[]{:S(2)}) async-start(), calls=%async_computation.3 | async-start | bytes 2621440 | tf_op jit(solution)/shard_map/reduce_scatter | solution.py:18
  8.3 54.8 %copy-start = (f32[1024,1024]{1,0:T(8,128)S(1)}, f32[1024,1024]{1,0:T(8,128)}, u32[]{:S(2)}) copy-start(f32[1024,1024]{1,0:T(8,128)} %param.7) | copy-start | bytes 12582916
  71.1 44.6 %copy-start.2 = (f32[256,1024]{1,0:T(8,128)S(1)}, f32[256,1024]{1,0:T(8,128)}, u32[]{:S(2)}) copy-start(f32[256,1024]{1,0:T(8,128)} %param.9) | copy-start | bytes 3145732
  71.1 68.5 %copy-start.3 = (f32[256,128]{1,0:T(8,128)S(1)}, f32[256,128]{1,0:T(8,128)}, u32[]{:S(2)}) copy-start(f32[256,128]{1,0:T(8,128)} %param.8) | copy-start | bytes 393220
  71.1 68.5 %reduce-scatter.5.cloned.1.call-start = ((), (), s32[]{:S(2)}) async-start(), calls=%async_computation.4 | async-start | bytes 655360 | tf_op jit(solution)/shard_map/reduce_scatter | solution.py:24
  207.9 0.7 copy-start.1
Sparse Core Ops, SparseCore 0:
  71.2 44.3 reduce-scatter.2
  118.2 21.1 reduce-scatter.4

commit v2 on v0

--- a/solution.py
+++ b/solution.py
@@ -14,7 +14,15 @@
     row_count = lax.axis_size("row")
     row_index = lax.axis_index("row")
     strip_rows = right_side.shape[0]
-    by_rows = lax.all_to_all(prev_solution, ("row", "col"), split_axis=0, concat_axis=1, tiled=True)
+    by_rows = jnp.concatenate(
+        lax.all_to_all(
+            jnp.stack(jnp.split(prev_solution, lax.axis_size(("row", "col")), axis=0)),
+            ("row", "col"),
+            0,
+            0,
+        ),
+        axis=1,
+    )
     row_summed = lax.psum_scatter(
         jnp.dot(factor_panel, by_rows, precision=highest, preferred_element_type=jnp.float32),
         "row",

time: 303 us -> 317 us (1.046)
  local copies, waits for them, and re-layouts: 6.83 us -> 20 us
    unnamed x9 -> x26, local copies, waits for them, and re-layouts: 0.76 us -> 14.7 us
where the time goes in v2:
time: 317 us; the launch traced here: 316 us
  waiting for transfers between devices  187 us (59%)
  blocking collectives  54.7 us (17%)
  other arithmetic  24.4 us (8%)
  local copies, waits for them, and re-layouts  20 us (6%)
  matrix products  16 us (5%)
  between operations  13.6 us (4%)
    psum x4, waiting for transfers between devices, broadcast(): return lax.psum(jnp.where(mine, value, jnp.zeros_like(value)), axis)  143 us
    all_to_all x1, blocking collectives, shards(): lax.all_to_all(jnp.stack(jnp.split(prev_solution, lax.axis_size(('row', '...  54.7 us
    reduce_scatter x1, waiting for transfers between devices, shards(): lax.psum_scatter(jnp.dot(factor_panel, by_rows, precision=highest, prefer...  44.4 us
    another operation x3, other arithmetic, sweep_step(): jax.scipy.linalg.solve_triangular(own_block, pending, lower=True)  19.7 us
    unnamed x26, local copies, waits for them, and re-layouts  14.7 us
    dot_general x1, matrix products, shards(): jnp.dot(factor_panel, by_rows, precision=highest, preferred_element_type=...  8.29 us
  transfers between devices with their start and end apart: 6, of which 5 were waited for; matrix products, arithmetic and copies ran while one was open for 8% of the time, Pallas kernels for 0%

profile of v2, /device:TPU:0, one launch (start us, length us, event | category | flops | bytes accessed | tf_op | source)
XLA Modules:
  0.0 316.4 jit_solution(12481545226899578860)
XLA Ops:
  7.5 0.9 bitcast_dynamic-update-slice_fusion.15
  8.4 0.9 bitcast_dynamic-update-slice_fusion.14
  9.3 0.9 bitcast_dynamic-update-slice_fusion.13
  10.2 0.9 bitcast_dynamic-update-slice_fusion.12
  11.1 0.9 bitcast_dynamic-update-slice_fusion.11
  12.1 0.9 bitcast_dynamic-update-slice_fusion.10
  13.0 0.9 bitcast_dynamic-update-slice_fusion.9
  13.9 0.9 bitcast_dynamic-update-slice_fusion.8
  14.8 0.9 bitcast_dynamic-update-slice_fusion.7
  15.7 0.9 bitcast_dynamic-update-slice_fusion.6
  16.7 0.9 bitcast_dynamic-update-slice_fusion.5
  17.6 0.9 bitcast_dynamic-update-slice_fusion.4
  18.5 0.9 bitcast_dynamic-update-slice_fusion.3
  19.4 0.9 bitcast_dynamic-update-slice_fusion.2
  21.3 54.7 %all_to_all.5 = f32[16,1024,32]{1,2,0:T(8,128)S(1)} all-to-all(f32[16,1024,32]{1,2,0:T(8,128)S(1)} %bitcast_dynamic-update-slice_fusion.1), channel_id=1, replica_groups=mesh['groups'=2,'row'=4,'col'=4] {'row','col'}, dimensions={0} | all-to-all | bytes 4194304 | tf_op jit(solution)/shard_map/all_to_all | solution.py:18
  76.0 8.3 %convolution_bitcast_fusion.1 = f32[1024,512]{0,1:T(8,128)} fusion(f32[1024,512]{0,1:T(8,128)S(1)} %bitcast.72, f32[1024,1024]{1,0:T(8,128)S(1)} %copy-done), kind=kOutput, calls=%fused_computation.24 | convolution fusion | flops 6442450944 | bytes 8388608 | tf_op jit(solution)/shard_map/dot_general | solution.py:27
  84.4 44.4 %reduce-scatter.3.cloned.1.call-done = f32[256,512]{0,1:T(8,128)} async-done(((f32[1024,512]{0,1:T(8,128)}), f32[256,512]{0,1:T(8,128)}) %reduce-scatter.3.cloned.1.call-update) | async-done | bytes 524304 | tf_op jit(solution)/shard_map/reduce_scatter | solution.py:26
  129.1 4.3 %while.20 = (s32[]{:T(128)}, f32[256,256]{1,0:T(8,128)S(1)}, s32[2,2]{1,0:T(2,128)S(1)}, f32[2,128,128]{2,1,0:T(8,128)S(1)}, s32[]{:T(128)}) while((s32[]{:T(128)}, f32[256,256]{1,0:T(8,128)S(1)}, s32[2,2]{1,0:T(2,128)S(1)}, f32[2,128,128]{2,1,0:T(8,128)S(1)}, s32[]{:T(128)}) %tuple.59), condition=%wide.while_cond, body=%wide.while_body.sunk | while | flops 2 | bytes 131189 | solution.py:38
  129.8 1.5 bitcast_dynamic-update-slice_fusion.18
  131.9 1.5 bitcast_dynamic-update-slice_fusion.18
  133.4 19.7 %custom-call.11 = f32[2,128,128]{1,2,0:T(8,128)S(1)} custom-call(f32[2,128,128]{2,1,0:T(8,128)S(1)} %get-tuple-element.195), custom_call_target="InvertDiagBlocksLowerTriangular" | custom-call | tf_op jit(solution)/shard_map/while/body/eval_jaxpr/jit(_solve_triangular)/triangular_solve | solution.py:38
  153.2 0.9 sub.13
  154.2 154.6 %while.21 = (s32[]{:T(128)}, f32[256,128]{1,0:T(8,128)S(1)}, f32[256,128]{1,0:T(8,128)S(1)}, s32[]{:T(128)}, f32[256,1024]{1,0:T(8,128)S(1)}, /*index=5*/f32[2,1...) while((s32[]{:T(128)}, f32[256,128]{1,0:T(8,128)S(1)}, ...), condition=%wide.region_4.5_spmd.clone, body=%wide.region_2.4_spmd.clone.sunk | while | flops 176472064 | bytes 2752807 | solution.py:50
  155.7 35.7 %all-reduce.2.cloned.1.call-done = f32[256,128]{1,0:T(8,128)} async-done(((f32[256,128]{1,0:T(8,128)}), f32[256,128]{1,0:T(8,128)}) %all-reduce.2.cloned.1.call-update) | async-done | bytes 131088 | tf_op jit(solution)/shard_map/while/body/eval_jaxpr/psum | solution.py:9
  191.3 1.3 fusion.41
  192.7 0.9 select_select_fusion.2
  195.0 34.6 %all-reduce.2.cloned.1.call-done = f32[256,128]{1,0:T(8,128)} async-done(((f32[256,128]{1,0:T(8,128)}), f32[256,128]{1,0:T(8,128)}) %all-reduce.2.cloned.1.call-update) | async-done | bytes 131088 | tf_op jit(solution)/shard_map/while/body/eval_jaxpr/psum | solution.py:9
  229.7 1.3 fusion.41
  232.5 35.8 %all-reduce.2.cloned.1.call-done = f32[256,128]{1,0:T(8,128)} async-done(((f32[256,128]{1,0:T(8,128)}), f32[256,128]{1,0:T(8,128)}) %all-reduce.2.cloned.1.call-update) | async-done | bytes 131088 | tf_op jit(solution)/shard_map/while/body/eval_jaxpr/psum | solution.py:9
  268.3 1.3 fusion.41
  271.1 36.4 %all-reduce.2.cloned.1.call-done = f32[256,128]{1,0:T(8,128)} async-done(((f32[256,128]{1,0:T(8,128)}), f32[256,128]{1,0:T(8,128)}) %all-reduce.2.cloned.1.call-update) | async-done | bytes 131088 | tf_op jit(solution)/shard_map/while/body/eval_jaxpr/psum | solution.py:9
  307.5 1.3 fusion.41
  (54 shorter events, 9.8 us)
Async XLA Ops:
  6.5 122.3 %reduce-scatter.3.cloned.1.call-start = ((), (), s32[]{:S(2)}) async-start(), calls=%async_computation.3 | async-start | bytes 2621440 | tf_op jit(solution)/shard_map/reduce_scatter | solution.py:26
  21.3 54.8 %copy-start = (f32[1024,1024]{1,0:T(8,128)S(1)}, f32[1024,1024]{1,0:T(8,128)}, u32[]{:S(2)}) copy-start(f32[1024,1024]{1,0:T(8,128)} %param.7) | copy-start | bytes 12582916
  84.3 44.5 %copy-start.3 = (f32[256,128]{1,0:T(8,128)S(1)}, f32[256,128]{1,0:T(8,128)}, u32[]{:S(2)}) copy-start(f32[256,128]{1,0:T(8,128)} %param.8) | copy-start | bytes 393220
  84.3 44.7 %copy-start.2 = (f32[256,1024]{1,0:T(8,128)S(1)}, f32[256,1024]{1,0:T(8,128)}, u32[]{:S(2)}) copy-start(f32[256,1024]{1,0:T(8,128)} %param.9) | copy-start | bytes 3145732
  84.3 68.9 %reduce-scatter.5.cloned.1.call-start = ((), (), s32[]{:S(2)}) async-start(), calls=%async_computation.4 | async-start | bytes 655360 | tf_op jit(solution)/shard_map/reduce_scatter | solution.py:32
  154.3 37.1 %all-reduce.2.cloned.1.call-start = ((), (), s32[]{:S(2)}) async-start(), calls=%async_computation.5 | async-start | bytes 262144 | tf_op jit(solution)/shard_map/while/body/eval_jaxpr/psum | solution.py:9
  193.6 36.0 %all-reduce.2.cloned.1.call-start = ((), (), s32[]{:S(2)}) async-start(), calls=%async_computation.5 | async-start | bytes 262144 | tf_op jit(solution)/shard_map/while/body/eval_jaxpr/psum | solution.py:9
  231.1 37.2 %all-reduce.2.cloned.1.call-start = ((), (), s32[]{:S(2)}) async-start(), calls=%async_computation.5 | async-start | bytes 262144 | tf_op jit(solution)/shard_map/while/body/eval_jaxpr/psum | solution.py:9
  269.7 37.8 %all-reduce.2.cloned.1.call-start = ((), (), s32[]{:S(2)}) async-start(), calls=%async_computation.5 | async-start | bytes 262144 | tf_op jit(solution)/shard_map/while/body/eval_jaxpr/psum | solution.py:9
  308.9 0.7 copy-start.1
Sparse Core Ops, SparseCore 0:
  84.5 44.2 reduce-scatter.2
  131.4 21.1 reduce-scatter.4
  157.4 33.8 all-reduce.1
  196.5 33.1 all-reduce.1
  233.9 34.3 all-reduce.1
  272.5 34.9 all-reduce.1
